TPU v7x, 512 devices: a whole 4x4x16 slice. The times are simulated.
512 devices in a mesh: grp: 32 (over z, x_lo), ep: 16 (over y, x_hi, core).
Axes of the slice: x: 4 (x_hi: 2, x_lo: 2; x = x_hi * 2 + x_lo), y: 4, z: 16, core: 2. Of those that a mesh axis runs over, the one named last changes fastest.
Arguments:
- hidden: bfloat16 [256, 1536], P('grp', 'ep'), may hold values from -12 to 12
- query: bfloat16 [256, 1536], P('grp'), may hold values from -16 to 16
- new_kv: bfloat16 [256, 2, 512], P('grp'), may hold values from -4 to 4
- key_cache: bfloat16 [98304, 512], P(('grp', 'ep')), may hold values from -6 to 6
- value_cache: bfloat16 [98304, 512], P(('grp', 'ep')), may hold values from -4 to 4
- page_owner: int32 [6144], P(('grp', 'ep')), may hold values from 0 to 15, as said below
- page_fill: int32 [6144], P(('grp', 'ep')), may hold values from 1 to 16, as said below
- out_weight: bfloat16 [1536, 1536], P('grp', 'ep'), may hold values from -0.75 to 0.75
- norm_gain: float32 [1536], P('ep'), may hold values from 0.25 to 1.75
- gate_up: bfloat16 [32, 1536, 1024], P('grp'), may hold values from -0.15625 to 0.15625
- down: bfloat16 [32, 512, 1536], P('grp'), may hold values from -0.25 to 0.25
- routes: int32 [256, 8], P('grp'), may hold values from 0 to 31, all different within a row; in each aligned block of 8 rows (0 to 7, 8 to 15, ...) at most 4 rows name the same one
- route_weight: bfloat16 [256, 8], P('grp'), may hold values from 0.049804688 to 0.3984375
Outputs:
- layer_out: bfloat16 [256, 1536], P('grp', 'ep')
- attn_out: bfloat16 [256, 1536], P('grp')
Inputs may be any that keep to these rules, and one draw needn't show every extreme that they name: `routes`: each row names 8 different experts. In each group's 8 rows (aligned blocks of 8 rows) no expert is named by more than 4 rows, a bound that some block reaches. `page_owner`: A value r under 8 names row r of the page's own group; a value 8 + r names row r of the partner group, whose index differs in the lowest bit. The first page_fill[p] tokens of page p are cached; the rest of the page is unused. The first page of every device is full.
All inputs are finite; a program needn't handle non-finite values.
Results may differ from a plain program's by a relative error of at most 0.017.
Values may be sent and summed in bfloat16 or wider, within the bound.
A program may use at most 64 MiB of HBM per device.

v0:
```python
import jax
import jax.numpy as jnp
from jax import lax
from jax.sharding import PartitionSpec as P

D = 1536
HEADS = 24
KV_HEADS = 8
HD = 64
FF = 512
TOP = 8
masked_score = -1e30
norm_epsilon = 1e-05


def from_partner(block, axis, apart):
    count = lax.axis_size(axis)
    route = []
    for low in range(count):
        high = low | 1 << apart
        if high != low and high < count:
            route += [(low, high), (high, low)]
    return lax.ppermute(block, axis, route)


def combined_all(part, axis, combine):
    gathered = jax.tree.map(lambda a: lax.all_gather(a, axis), part)

    def take(source):
        return jax.tree.map(lambda a: lax.dynamic_index_in_dim(a, source, 0, False), gathered)

    return lax.fori_loop(
        1, lax.axis_size(axis), lambda source, state: combine(state, take(source)), take(0)
    )


def merge_parts(earlier, later):
    max_one, total_one, accum_one = earlier
    max_two, total_two, accum_two = later
    highest = jnp.maximum(max_one, max_two)
    factor_one = jnp.exp(max_one - highest)
    factor_two = jnp.exp(max_two - highest)
    return (
        highest,
        total_one * factor_one + total_two * factor_two,
        accum_one * factor_one[..., None] + accum_two * factor_two[..., None],
    )


def per_device(
    hidden,
    query,
    new_kv,
    key_cache,
    value_cache,
    page_owner,
    page_fill,
    out_weight,
    norm_gain,
    gate_up,
    down,
    routes,
    route_weight,
):
    row_count = query.shape[0]
    group_count = lax.axis_size("grp")
    head_group = HEADS // KV_HEADS
    page_count = page_owner.shape[0]
    token_count = key_cache.shape[0]
    page_length = token_count // page_count
    both_rows = 2 * row_count
    scale = HD ** (-0.5)
    partner_query = from_partner(query, "grp", 0)
    all_queries = jnp.concatenate([query, partner_query], 0)
    query_heads = (
        all_queries.reshape(both_rows, KV_HEADS, head_group, HD)
        .transpose(1, 0, 2, 3)
        .reshape(KV_HEADS, both_rows * head_group, HD)
    )
    key_heads = key_cache.reshape(token_count, KV_HEADS, HD)
    value_heads = value_cache.reshape(token_count, KV_HEADS, HD)
    scores = (
        jnp.einsum("kqd,tkd->kqt", query_heads, key_heads, preferred_element_type=jnp.float32)
        * scale
    )
    scores = scores.reshape(KV_HEADS, both_rows, head_group, token_count)
    row_index = jnp.arange(both_rows, dtype=jnp.int32)
    in_page = jnp.arange(page_length, dtype=jnp.int32)
    usable = (page_owner[None, :, None] == row_index[:, None, None]) & (
        in_page[None, None, :] < page_fill[None, :, None]
    )
    usable = usable.reshape(both_rows, token_count)[None, :, None, :]
    local_top = jnp.max(jnp.where(usable, scores, masked_score), -1)
    weights = jnp.where(usable, jnp.exp(scores - local_top[..., None]), 0.0)
    local_total = jnp.sum(weights, -1)
    rounded = weights.astype(jnp.bfloat16).reshape(KV_HEADS, both_rows * head_group, token_count)
    local_accum = jnp.einsum(
        "kqt,tkd->kqd", rounded, value_heads, preferred_element_type=jnp.float32
    )
    part_max = local_top.transpose(1, 0, 2).reshape(both_rows, HEADS)
    part_total = local_total.transpose(1, 0, 2).reshape(both_rows, HEADS)
    part_accum = (
        local_accum.reshape(KV_HEADS, both_rows, head_group, HD)
        .transpose(1, 0, 2, 3)
        .reshape(both_rows, HEADS, HD)
    )
    merged = combined_all((part_max, part_total, part_accum), "ep", merge_parts)
    returned = from_partner(
        (merged[0][row_count:], merged[1][row_count:], merged[2][row_count:]), "grp", 0
    )
    combined = merge_parts(
        (merged[0][:row_count], merged[1][:row_count], merged[2][:row_count]), returned
    )
    own_query = query.reshape(row_count, KV_HEADS, head_group, HD)
    fresh_key = new_kv[:, 0].reshape(row_count, KV_HEADS, HD)
    fresh_value = new_kv[:, 1].astype(jnp.float32).reshape(row_count, KV_HEADS, HD)
    own_score = (
        jnp.einsum(
            "rkgd,rkd->rkg", own_query, fresh_key, preferred_element_type=jnp.float32
        ).reshape(row_count, HEADS)
        * scale
    )
    cache_max, cache_total, cache_accum = combined
    highest = jnp.maximum(cache_max, own_score)
    cache_factor = jnp.exp(cache_max - highest)
    own_weight = jnp.exp(own_score - highest)
    value_rows = jnp.broadcast_to(
        fresh_value[:, :, None, :], (row_count, KV_HEADS, head_group, HD)
    ).reshape(row_count, HEADS, HD)
    numerator = cache_accum * cache_factor[..., None] + own_weight[..., None] * value_rows
    denominator = cache_total * cache_factor + own_weight
    attn_out = (
        (numerator / denominator[..., None]).reshape(row_count, HEADS * HD).astype(jnp.bfloat16)
    )
    head_share = out_weight.shape[0]
    feature_share = hidden.shape[1]
    every_head = lax.all_gather(attn_out, "grp", axis=0, tiled=True)
    head_columns = lax.dynamic_slice_in_dim(
        every_head, lax.axis_index("grp") * head_share, head_share, 1
    )
    projected = lax.psum_scatter(
        jnp.dot(head_columns, out_weight, preferred_element_type=jnp.float32).astype(jnp.bfloat16),
        "grp",
        scatter_dimension=0,
        tiled=True,
    ).astype(jnp.float32)
    mixed = hidden.astype(jnp.float32) + projected
    squares = lax.psum(jnp.sum(mixed * mixed, -1), "ep")
    normed = (mixed * lax.rsqrt(squares / D + norm_epsilon)[:, None] * norm_gain).astype(
        jnp.bfloat16
    )
    capacity = min(row_count, 2 * row_count * TOP // group_count)
    expert_ids = jnp.arange(group_count, dtype=jnp.int32)
    flat_routes = routes.reshape(-1)
    hits = (flat_routes[:, None] == expert_ids[None, :]).astype(jnp.int32)
    earlier_hits = jnp.cumsum(hits, 0) - hits
    position = jnp.sum(earlier_hits * hits, 1)
    slot_index = flat_routes * capacity + position
    slots_all = jnp.arange(group_count * capacity, dtype=jnp.int32)
    picker = jnp.any(
        slot_index.reshape(row_count, TOP)[None, :, :] == slots_all[:, None, None], 2
    ).astype(jnp.bfloat16)
    sender = (
        jnp.dot(picker, normed, preferred_element_type=jnp.float32)
        .astype(jnp.bfloat16)
        .reshape(group_count, capacity, feature_share)
    )
    arrived = lax.all_to_all(sender, "grp", split_axis=0, concat_axis=0, tiled=True)
    whole_rows = lax.all_to_all(
        arrived.reshape(group_count * capacity, feature_share),
        "ep",
        split_axis=0,
        concat_axis=1,
        tiled=True,
    )
    pre_sum = jnp.dot(whole_rows, gate_up[0], preferred_element_type=jnp.float32)
    activated = (jax.nn.silu(pre_sum[:, :FF]) * pre_sum[:, FF:]).astype(jnp.bfloat16)
    result = jnp.dot(activated, down[0], preferred_element_type=jnp.float32).astype(jnp.bfloat16)
    served = lax.all_to_all(result, "ep", split_axis=1, concat_axis=0, tiled=True).reshape(
        group_count, capacity, feature_share
    )
    returned_rows = lax.all_to_all(served, "grp", split_axis=0, concat_axis=0, tiled=True)
    gathered_rows = returned_rows.reshape(group_count * capacity, feature_share)[
        slot_index
    ].reshape(row_count, TOP, feature_share)
    expert_mix = jnp.sum(
        route_weight.astype(jnp.float32)[:, :, None] * gathered_rows.astype(jnp.float32), 1
    )
    layer_out = (mixed + expert_mix).astype(jnp.bfloat16)
    return (layer_out, attn_out)


def solution(mesh):
    placed = (
        P("grp", "ep"),
        P("grp", None),
        P("grp", None, None),
        P(("grp", "ep"), None),
        P(("grp", "ep"), None),
        P(("grp", "ep")),
        P(("grp", "ep")),
        P("grp", "ep"),
        P("ep"),
        P("grp", None, None),
        P("grp", None, None),
        P("grp", None),
        P("grp", None),
    )
    return jax.shard_map(
        per_device,
        mesh=mesh,
        in_specs=placed,
        out_specs=(P("grp", "ep"), P("grp", None)),
        check_vma=False,
    )
```

profile of v0, /device:TPU:1, one launch (start us, length us, event | category | flops | bytes accessed | tf_op | source)
XLA Modules:
  0.0 435.2 jit_solution(1514925168340241131)
XLA Ops:
  7.2 4.2 collective-permute-start
  13.3 1.8 copy.96
  15.1 1.8 copy.104
  17.8 1.2 select_reduce_fusion
  19.0 1.2 fusion.8
  21.1 1.5 reshape.181
  22.6 1.4 slice_reduce_fusion
  24.0 1.4 reshape.199
  25.3 1.7 fusion.43
  27.0 1.5 copy.120
  28.5 1.3 bitcast_multiply_fusion.3
  29.8 1.3 mul.194
  31.1 1.4 convert_reduce_fusion
  32.5 1.4 reshape.186
  33.9 1.4 copy.112
  35.3 1.3 eq.49
  36.5 1.3 fusion.21
  37.9 1.4 reduce_window_sum.11
  39.3 1.4 select_reduce_fusion.1
  40.7 1.2 reduce_sum.45
  42.0 1.3 broadcast_multiply_fusion
  46.7 25.4 %all_gather.13 = f32[16,16,24]{2,1,0:T(8,128)S(1)} all-gather(f32[1,16,24]{2,1,0:T(8,128)S(1)} %copy.103), channel_id=1, replica_groups=mesh['grp'=32,'ep'=16] {'ep'}, dimensions={0}, use_global_device_ids=true | all-gather | bytes 26112 | tf_op jit(solution)/shard_map/all_gather | solution.py:27
  72.1 22.3 %all_gather.12 = f32[16,16,24]{2,1,0:T(8,128)S(1)} all-gather(f32[1,16,24]{2,1,0:T(8,128)S(1)} %copy.100), channel_id=1, replica_groups=mesh['grp'=32,'ep'=16] {'ep'}, dimensions={0}, use_global_device_ids=true | all-gather | bytes 26112 | tf_op jit(solution)/shard_map/all_gather | solution.py:27
  96.0 28.2 %while.19 = (s32[]{:T(128)}, f32[16,24]{1,0:T(8,128)S(1)}, f32[16,24]{1,0:T(8,128)S(1)}, f32[16,24,64]{2,1,0:T(8,128)S(1)}, f32[16,16,24]{2,1,0:T(8,128)}, /*ind...) while((s32[]{:T(128)}, f32[16,24]{1,0:T(8,128)S(1)}, ...), condition=%wide.region_3.4_spmd, body=%wide.region_2.3_spmd.sunk | while | flops 76037 | bytes 310423 | solution.py:32
  96.7 1.1 fusion.54
  98.6 1.1 fusion.54
  100.5 1.1 fusion.54
  102.3 1.1 fusion.54
  108.0 1.1 fusion.54
  113.6 1.1 fusion.54
  115.5 1.1 fusion.54
  121.1 1.1 fusion.54
  123.0 1.1 fusion.54
  124.3 3.6 collective-permute-start.1
  128.7 1.9 collective-permute-start.3
  130.6 1.3 dynamic-slice
  132.6 3.4 collective-permute-start.2
  136.8 1.7 collective-permute-done.2
  138.8 55.3 %all_gather.15 = bf16[256,1536]{1,0:T(8,128)(2,1)S(1)} all-gather(bf16[8,1536]{1,0:T(8,128)(2,1)S(1)} %convert_element_type.62), channel_id=1, replica_groups=mesh['grp'=32,'ep'=16] {'grp'}, dimensions={0}, use_global_device_ids=true | all-gather | bytes 811008 | tf_op jit(solution)/shard_map/all_gather | solution.py:137
  194.3 91.1 %all-reduce = bf16[256,96]{1,0:T(8,128)(2,1)S(1)} all-reduce(bf16[256,96]{1,0:T(8,128)(2,1)S(1)} %convolution_convert_fusion.1), channel_id=2, replica_groups=mesh['grp'=32,'ep'=16] {'grp'}, use_global_device_ids=true, to_apply=%region_4.5.clone | all-reduce | flops 24576 | bytes 98304
  286.3 75.5 %psum.7 = f32[8]{0:T(128)S(1)} all-reduce(f32[8]{0:T(128)S(1)} %multiply_reduce_fusion), channel_id=1, replica_groups=mesh['grp'=32,'ep'=16] {'ep'}, use_global_device_ids=true, to_apply=%region_9.10 | all-reduce | flops 8 | bytes 64 | tf_op jit(solution)/shard_map/psum | solution.py:148
  362.9 21.1 %all_to_all.45 = bf16[32,4,96]{2,1,0:T(4,128)(2,1)} all-to-all(bf16[32,4,96]{2,1,0:T(4,128)(2,1)S(1)} %bitcast.92), channel_id=1, replica_groups=mesh['grp'=32,'ep'=16] {'grp'}, dimensions={0} | all-to-all | bytes 49152 | tf_op jit(solution)/shard_map/all_to_all | solution.py:168
  384.0 5.4 %all-to-all-start.1 = ((bf16[16,8,96]{2,1,0:T(8,128)(2,1)}), bf16[16,8,96]{2,1,0:T(8,128)(2,1)S(1)}, u32[]{:S(2)}, u32[]{:S(2)}) async-start(bf16[16,8,96]{2,1,0:T(8,128)(2,1)} %bitcast.18), calls=%async_computation.1 | async-start | bytes 65536 | tf_op jit(solution)/shard_map/all_to_all | solution.py:169
  389.4 7.3 %all-to-all-done.1 = bf16[16,8,96]{2,1,0:T(8,128)(2,1)S(1)} async-done(((bf16[16,8,96]{2,1,0:T(8,128)(2,1)}), bf16[16,8,96]{2,1,0:T(8,128)(2,1)S(1)}, u32[]{:S(2)}, u32[]{:S(2)}) %all-to-all-start.1) | async-done | bytes 24608 | tf_op jit(solution)/shard_map/all_to_all | solution.py:169
  399.3 4.2 all-to-all-start.2
  403.5 7.4 %all-to-all-done.2 = bf16[8,16,96]{2,0,1:T(8,128)(2,1)} async-done(((bf16[8,16,96]{2,0,1:T(8,128)(2,1)}), bf16[8,16,96]{2,0,1:T(8,128)(2,1)}, u32[]{:S(2)}, u32[]{:S(2)}) %all-to-all-start.2) | async-done | bytes 24608 | tf_op jit(solution)/shard_map/all_to_all | solution.py:179
  411.0 3.9 all-to-all-start.3
  414.8 12.2 %all-to-all-done.3 = bf16[32,4,96]{2,1,0:T(4,128)(2,1)S(1)} async-done(((bf16[32,4,96]{2,1,0:T(4,128)(2,1)}), bf16[32,4,96]{2,1,0:T(4,128)(2,1)S(1)}, u32[]{:S(2)}, u32[]{:S(2)}) %all-to-all-start.3) | async-done | bytes 24608 | tf_op jit(solution)/shard_map/all_to_all | solution.py:182
  (111 shorter events, 34.4 us)
Async XLA Ops:
  7.2 389.6 %copy-start = (bf16[1,1536,1024]{2,1,0:T(8,128)(2,1)S(1)}, bf16[1,1536,1024]{2,1,0:T(8,128)(2,1)}, u32[]{:S(2)}) copy-start(bf16[1,1536,1024]{2,1,0:T(8,128)(2,1)} %param.24) | copy-start | bytes 9437188
  7.2 87.8 %all-gather.2.cloned.1.call-start = ((), (), s32[]{:S(2)}) async-start(), calls=%async_computation.4 | async-start | bytes 3342336 | tf_op jit(solution)/shard_map/all_gather | solution.py:27
  7.2 9.6 %collective-permute-start = (bf16[8,1536]{1,0:T(8,128)(2,1)}, bf16[8,1536]{1,0:T(8,128)(2,1)S(1)}, u32[]{:S(2)}, u32[]{:S(2)}) collective-permute-start(bf16[8,1536]{1,0:T(8,128)(2,1)} %param.16), channel_id=1, source_target_pairs={{0,16},{16,0},{32,48},{48,32},{64,80},{80,64},{96,112},{112,96},{1... | collective-permute-start | bytes 73736 | tf_op jit(solution)/shard_map/ppermute | solution.py:23
  44.8 91.2 %copy-start.5 = (f32[8,24]{0,1:T(8,128)S(1)}, f32[8,24]{0,1:T(8,128)}, u32[]{:S(2)}) copy-start(f32[8,24]{0,1:T(8,128)} %mul.194) | copy-start | bytes 2308
  44.8 93.6 %copy-start.3 = (f32[8,8,64]{2,0,1:T(8,128)S(1)}, f32[8,8,64]{2,0,1:T(8,128)}, u32[]{:S(2)}) copy-start(f32[8,8,64]{2,0,1:T(8,128)} %copy.112) | copy-start | bytes 49156
  72.1 122.0 %copy-start.8 = (bf16[48,96]{1,0:T(8,128)(2,1)S(1)}, bf16[48,96]{1,0:T(8,128)(2,1)}, u32[]{:S(2)}) copy-start(bf16[48,96]{1,0:T(8,128)(2,1)} %param.22) | copy-start | bytes 27652
  94.4 0.6 copy-start.2
  95.0 191.1 %copy-start.6 = (s32[8,8]{1,0:T(8,128)S(1)}, s32[8,8]{1,0:T(8,128)}, u32[]{:S(2)}) copy-start(s32[8,8]{1,0:T(8,128)} %get-tuple-element.221) | copy-start | bytes 772
  96.0 293.4 %copy-start.7 = (s32[8,8]{1,0:T(8,128)S(1)}, s32[8,8]{1,0:T(8,128)}, u32[]{:S(2)}) copy-start(s32[8,8]{1,0:T(8,128)} %get-tuple-element.220) | copy-start | bytes 772
  124.3 11.7 %collective-permute-start.1 = (f32[8,24]{0,1:T(8,128)S(1)}, f32[8,24]{0,1:T(8,128)}, u32[]{:S(2)}, u32[]{:S(2)}) collective-permute-start(f32[8,24]{0,1:T(8,128)S(1)} %slice.47), channel_id=1, source_target_pairs={{0,16},{16,0},{32,48},{48,32},{64,80},{80,64},{96,112},{112,96},{1... | collective-permute-start | bytes 2312 | tf_op jit(solution)/shard_map/ppermute | solution.py:23
  128.7 7.3 %collective-permute-start.3 = (f32[8,24]{0,1:T(8,128)}, f32[8,24]{0,1:T(8,128)}, u32[]{:S(2)}, u32[]{:S(2)}) collective-permute-start(f32[8,24]{0,1:T(8,128)} %slice.50), channel_id=1, source_target_pairs={{0,16},{16,0},{32,48},{48,32},{64,80},{80,64},{96,112},{112,96},{1... | collective-permute-start | bytes 2312 | tf_op jit(solution)/shard_map/ppermute | solution.py:23
  132.6 5.8 %collective-permute-start.2 = (f32[8,24,64]{2,0,1:T(8,128)S(1)}, f32[8,24,64]{2,0,1:T(8,128)S(1)}, u32[]{:S(2)}, u32[]{:S(2)}) collective-permute-start(f32[8,24,64]{2,0,1:T(8,128)S(1)} %slice.48), channel_id=1, source_target_pairs={{0,16},{16,0},{32,48},{48,32},{64,80},{80,64},{96,112},{112,96},{1... | collective-permute-start | bytes 147464 | tf_op jit(solution)/shard_map/ppermute | solution.py:23
  138.8 259.8 %copy-start.4 = (bf16[8,1536]{1,0:T(8,128)(2,1)}, bf16[8,1536]{1,0:T(8,128)(2,1)S(1)}, u32[]{:S(2)}) copy-start(bf16[8,1536]{1,0:T(8,128)(2,1)S(1)} %convert_element_type.62) | copy-start | bytes 73732
  138.8 264.7 %copy-start.10 = (s32[64]{0:T(128)S(1)}, s32[64]{0:T(128)}, u32[]{:S(2)}) copy-start(s32[64]{0:T(128)} %select_reduce_fusion.1) | copy-start | bytes 772
  138.8 264.7 %copy-start.11 = (bf16[8,8]{1,0:T(8,128)(2,1)S(1)}, bf16[8,8]{1,0:T(8,128)(2,1)}, u32[]{:S(2)}) copy-start(bf16[8,8]{1,0:T(8,128)(2,1)} %param.27) | copy-start | bytes 388
  194.1 233.7 %copy-start.9 = (bf16[8,96]{1,0:T(8,128)(2,1)S(1)}, bf16[8,96]{1,0:T(8,128)(2,1)}, u32[]{:S(2)}) copy-start(bf16[8,96]{1,0:T(8,128)(2,1)} %param.15) | copy-start | bytes 4612
  384.0 12.7 %all-to-all-start.1 = ((bf16[16,8,96]{2,1,0:T(8,128)(2,1)}), bf16[16,8,96]{2,1,0:T(8,128)(2,1)S(1)}, u32[]{:S(2)}, u32[]{:S(2)}) async-start(bf16[16,8,96]{2,1,0:T(8,128)(2,1)} %bitcast.18), calls=%async_computation.1 | async-start | bytes 65536 | tf_op jit(solution)/shard_map/all_to_all | solution.py:169
  396.8 1.4 copy-start.1
  399.3 11.7 %all-to-all-start.2 = ((bf16[8,16,96]{2,0,1:T(8,128)(2,1)}), bf16[8,16,96]{2,0,1:T(8,128)(2,1)}, u32[]{:S(2)}, u32[]{:S(2)}) async-start(bf16[8,16,96]{2,0,1:T(8,128)(2,1)} %copy.118), calls=%async_computation.2 | async-start | bytes 65536 | tf_op jit(solution)/shard_map/all_to_all | solution.py:179
  411.0 16.1 %all-to-all-start.3 = ((bf16[32,4,96]{2,1,0:T(4,128)(2,1)}), bf16[32,4,96]{2,1,0:T(4,128)(2,1)S(1)}, u32[]{:S(2)}, u32[]{:S(2)}) async-start(bf16[32,4,96]{2,1,0:T(4,128)(2,1)} %bitcast.23), calls=%async_computation.3 | async-start | bytes 65536 | tf_op jit(solution)/shard_map/all_to_all | solution.py:182
Sparse Core Ops, SparseCore 0:
  21.2 71.9 all-gather.1
where the time goes:
time: 438 us; the launch traced here: 435 us
  blocking collectives  291 us (66%)
  other arithmetic  40.8 us (9%)
  waiting for transfers between devices  28.6 us (7%)
  local copies, waits for them, and re-layouts  27.1 us (6%)
  starting transfers between devices  26.6 us (6%)
  between operations  15 us (3%)
  matrix products  6.08 us (1%)
    unnamed x1, blocking collectives  91.1 us
    psum x1, blocking collectives, per_device(): squares = lax.psum(jnp.sum(mixed * mixed, -1), 'ep')  75.5 us
    all_gather x1, blocking collectives, per_device(): every_head = lax.all_gather(attn_out, 'grp', axis=0, tiled=True)  55.3 us
    all_gather x2, blocking collectives, combined_all(): gathered = jax.tree.map(lambda a: lax.all_gather(a, axis), part)  47.7 us
    all_to_all x1, blocking collectives, per_device(): lax.all_to_all(sender, 'grp', split_axis=0, concat_axis=0, tiled=True)  21.1 us
    add x15, other arithmetic, merge_parts(): accum_one * factor_one[..., None] + accum_two * factor_two[..., None]  17 us
    ppermute x4, starting transfers between devices, from_partner(): return lax.ppermute(block, axis, route)  13.1 us
    all_to_all x1, waiting for transfers between devices, per_device(): lax.all_to_all(served, 'grp', split_axis=0, concat_axis=0, tiled=True)  12.2 us
  transfers between devices with their start and end apart: 8, of which 4 were waited for; matrix products, arithmetic and copies ran while one was open for 8% of the time, Pallas kernels for 0%

commit v1 on v0

--- a/solution.py
+++ b/solution.py
@@ -11,6 +11,13 @@
 TOP = 8
 masked_score = -1e30
 norm_epsilon = 1e-05
+
+
+def exchange_gather(value, axis, along):
+    size = lax.axis_size(axis)
+    tiles = jnp.stack([value for _ in range(size)])
+    tiles = lax.all_to_all(tiles, axis, split_axis=0, concat_axis=0)
+    return jnp.concatenate(tiles, axis=along)
 
 
 def from_partner(block, axis, apart):
@@ -134,7 +141,7 @@
     )
     head_share = out_weight.shape[0]
     feature_share = hidden.shape[1]
-    every_head = lax.all_gather(attn_out, "grp", axis=0, tiled=True)
+    every_head = exchange_gather(attn_out, "grp", 0)
     head_columns = lax.dynamic_slice_in_dim(
         every_head, lax.axis_index("grp") * head_share, head_share, 1
     )

time: 438 us -> 416 us (0.950)
  blocking collectives: 291 us -> 219 us
  waiting for transfers between devices: 28.6 us -> 80.4 us
  starting transfers between devices: 26.6 us -> 38 us
  other arithmetic: 40.8 us -> 32.9 us
  local copies, waits for them, and re-layouts: 27.1 us -> 21.1 us
    all_gather x1 -> x0, blocking collectives: 55.3 us -> none  [per_device(): every_head = lax.all_gather(attn_out, 'grp', axis=0, tiled=True)]
    all_to_all x0 -> x1, waiting for transfers between devices: none -> 39.1 us  [exchange_gather(): tiles = lax.all_to_all(tiles, axis, split_axis=0, concat_axis=0)]
    all_to_all x0 -> x1, starting transfers between devices: none -> 12.8 us  [exchange_gather(): tiles = lax.all_to_all(tiles, axis, split_axis=0, concat_axis=0)]
    all_gather x1, waiting for transfers between devices: 0.01 us -> 11.2 us  [combined_all(): gathered = jax.tree.map(lambda a: lax.all_gather(a, axis), part)]
    psum x1, blocking collectives: 75.5 us -> 64.7 us  [per_device(): squares = lax.psum(jnp.sum(mixed * mixed, -1), 'ep')]
    all_to_all x1, blocking collectives: 21.1 us -> 16.1 us  [per_device(): lax.all_to_all(sender, 'grp', split_axis=0, concat_axis=0, tiled=True)]
  transfers between devices with their start and end apart: 8 -> 9, of which waited for: 4 -> 6; matrix products, arithmetic and copies ran while one was open for 8% -> 5% of each run, Pallas kernels for 0% -> 0%
where the time goes in v1:
time: 416 us; the launch traced here: 413 us
  blocking collectives  219 us (53%)
  waiting for transfers between devices  80.4 us (19%)
  starting transfers between devices  38 us (9%)
  other arithmetic  32.9 us (8%)
  local copies, waits for them, and re-layouts  21.1 us (5%)
  between operations  15.1 us (4%)
  matrix products  6.28 us (2%)
    unnamed x1, blocking collectives  91.1 us
    psum x1, blocking collectives, per_device(): squares = lax.psum(jnp.sum(mixed * mixed, -1), 'ep')  64.7 us
    all_gather x2, blocking collectives, combined_all(): gathered = jax.tree.map(lambda a: lax.all_gather(a, axis), part)  47.3 us
    all_to_all x1, waiting for transfers between devices, exchange_gather(): tiles = lax.all_to_all(tiles, axis, split_axis=0, concat_axis=0)  39.1 us
    add x15, other arithmetic, merge_parts(): accum_one * factor_one[..., None] + accum_two * factor_two[..., None]  17 us
    all_to_all x1, blocking collectives, per_device(): lax.all_to_all(sender, 'grp', split_axis=0, concat_axis=0, tiled=True)  16.1 us
    all_to_all x1, starting transfers between devices, exchange_gather(): tiles = lax.all_to_all(tiles, axis, split_axis=0, concat_axis=0)  12.8 us
    all_to_all x1, waiting for transfers between devices, per_device(): lax.all_to_all(served, 'grp', split_axis=0, concat_axis=0, tiled=True)  12.2 us
  transfers between devices with their start and end apart: 9, of which 6 were waited for; matrix products, arithmetic and copies ran while one was open for 5% of the time, Pallas kernels for 0%

profile of v1, /device:TPU:1, one launch (start us, length us, event | category | flops | bytes accessed | tf_op | source)
XLA Modules:
  0.0 413.3 jit_solution(9160027082870541531)
XLA Ops:
  7.2 4.2 %collective-permute-start = (bf16[8,1536]{1,0:T(8,128)(2,1)}, bf16[8,1536]{1,0:T(8,128)(2,1)S(1)}, u32[]{:S(2)}, u32[]{:S(2)}) collective-permute-start(bf16[8,1536]{1,0:T(8,128)(2,1)} %param.16), channel_id=1, source_target_pairs={{0,16},{16,0},{32,48},{48,32},{64,80},{80,64},{96,112},{112,96},{1... | collective-permute-start | bytes 73736 | tf_op jit(solution)/shard_map/ppermute | solution.py:30
  13.3 1.8 copy.96
  15.1 1.8 copy.104
  17.8 1.2 select_reduce_fusion
  19.0 1.2 fusion.8
  21.1 1.5 reshape.187
  22.6 1.4 slice_reduce_fusion
  24.0 1.4 reshape.206
  25.3 1.7 fusion.43
  27.0 1.5 copy.120
  28.5 1.3 bitcast_multiply_fusion.3
  33.2 25.6 %all_gather.10 = f32[16,16,24]{2,1,0:T(8,128)S(1)} all-gather(f32[1,16,24]{2,1,0:T(8,128)S(1)} %copy.103), channel_id=1, replica_groups=mesh['grp'=32,'ep'=16] {'ep'}, dimensions={0}, use_global_device_ids=true | all-gather | bytes 26112 | tf_op jit(solution)/shard_map/all_gather | solution.py:34
  58.8 21.7 %all_gather.9 = f32[16,16,24]{2,1,0:T(8,128)S(1)} all-gather(f32[1,16,24]{2,1,0:T(8,128)S(1)} %copy.100), channel_id=1, replica_groups=mesh['grp'=32,'ep'=16] {'ep'}, dimensions={0}, use_global_device_ids=true | all-gather | bytes 26112 | tf_op jit(solution)/shard_map/all_gather | solution.py:34
  81.1 11.2 %all-gather.2.cloned.1.call-done = f32[16,16,24,64]{3,2,1,0:T(8,128)} async-done(((f32[1,16,24,64]{3,2,1,0:T(8,128)}), f32[16,16,24,64]{3,2,1,0:T(8,128)}) %all-gather.2.cloned.1.call-update) | async-done | bytes 1572880 | tf_op jit(solution)/shard_map/all_gather | solution.py:34
  93.3 28.1 %while.19 = (s32[]{:T(128)}, f32[16,24]{1,0:T(8,128)S(1)}, f32[16,24]{1,0:T(8,128)S(1)}, f32[16,24,64]{2,1,0:T(8,128)S(1)}, f32[16,16,24]{2,1,0:T(8,128)}, /*ind...) while((s32[]{:T(128)}, f32[16,24]{1,0:T(8,128)S(1)}, ...), condition=%wide.region_3.4_spmd, body=%wide.region_2.3_spmd.sunk | while | flops 76037 | bytes 310423 | solution.py:39
  94.0 1.1 fusion.54
  95.9 1.1 fusion.54
  97.8 1.1 fusion.54
  99.7 1.1 fusion.54
  101.5 1.1 fusion.54
  103.4 1.1 fusion.54
  105.3 1.1 fusion.54
  107.2 1.1 fusion.54
  109.0 1.1 fusion.54
  110.9 1.1 fusion.54
  112.8 1.1 fusion.54
  114.7 1.1 fusion.54
  116.5 1.1 fusion.54
  118.4 1.1 fusion.54
  120.3 1.1 fusion.54
  121.6 2.2 collective-permute-start.1
  123.9 3.1 collective-permute-start.3
  127.3 2.2 collective-permute-start.2
  129.5 3.1 collective-permute-done.2
  133.0 1.0 stack.2
  133.9 12.8 %all-to-all-start = ((bf16[32,8,1536]{2,1,0:T(8,128)(2,1)}), bf16[32,8,1536]{2,1,0:T(8,128)(2,1)}, u32[]{:S(2)}, u32[]{:S(2)}) async-start(bf16[32,8,1536]{2,1,0:T(8,128)(2,1)} %stack.2), calls=%async_computation | async-start | bytes 1572864 | tf_op jit(solution)/shard_map/all_to_all | solution.py:19
  147.3 1.3 dynamic-slice
  149.3 39.1 %all-to-all-done = bf16[32,8,1536]{2,1,0:T(8,128)(2,1)} async-done(((bf16[32,8,1536]{2,1,0:T(8,128)(2,1)}), bf16[32,8,1536]{2,1,0:T(8,128)(2,1)}, u32[]{:S(2)}, u32[]{:S(2)}) %all-to-all-start) | async-done | bytes 786464 | tf_op jit(solution)/shard_map/all_to_all | solution.py:19
  188.4 1.1 convolution_convert_fusion.1
  189.5 91.1 %all-reduce = bf16[256,96]{1,0:T(8,128)(2,1)S(1)} all-reduce(bf16[256,96]{1,0:T(8,128)(2,1)S(1)} %convolution_convert_fusion.1), channel_id=2, replica_groups=mesh['grp'=32,'ep'=16] {'grp'}, use_global_device_ids=true, to_apply=%region_4.5.clone | all-reduce | flops 24576 | bytes 98304
  280.8 64.7 %psum.7 = f32[8]{0:T(128)S(1)} all-reduce(f32[8]{0:T(128)S(1)} %multiply_reduce_fusion), channel_id=1, replica_groups=mesh['grp'=32,'ep'=16] {'ep'}, use_global_device_ids=true, to_apply=%region_9.10 | all-reduce | flops 8 | bytes 64 | tf_op jit(solution)/shard_map/psum | solution.py:155
  345.9 16.1 %all_to_all.50 = bf16[32,4,96]{2,1,0:T(4,128)(2,1)} all-to-all(bf16[32,4,96]{2,1,0:T(4,128)(2,1)S(1)} %bitcast.93), channel_id=1, replica_groups=mesh['grp'=32,'ep'=16] {'grp'}, dimensions={0} | all-to-all | bytes 49152 | tf_op jit(solution)/shard_map/all_to_all | solution.py:175
  362.1 5.4 %all-to-all-start.2 = ((bf16[16,8,96]{2,1,0:T(8,128)(2,1)}), bf16[16,8,96]{2,1,0:T(8,128)(2,1)S(1)}, u32[]{:S(2)}, u32[]{:S(2)}) async-start(bf16[16,8,96]{2,1,0:T(8,128)(2,1)} %bitcast.19), calls=%async_computation.2 | async-start | bytes 65536 | tf_op jit(solution)/shard_map/all_to_all | solution.py:176
  367.5 7.3 %all-to-all-done.2 = bf16[16,8,96]{2,1,0:T(8,128)(2,1)S(1)} async-done(((bf16[16,8,96]{2,1,0:T(8,128)(2,1)}), bf16[16,8,96]{2,1,0:T(8,128)(2,1)S(1)}, u32[]{:S(2)}, u32[]{:S(2)}) %all-to-all-start.2) | async-done | bytes 24608 | tf_op jit(solution)/shard_map/all_to_all | solution.py:176
  377.4 4.2 %all-to-all-start.3 = ((bf16[8,16,96]{2,0,1:T(8,128)(2,1)}), bf16[8,16,96]{2,0,1:T(8,128)(2,1)}, u32[]{:S(2)}, u32[]{:S(2)}) async-start(bf16[8,16,96]{2,0,1:T(8,128)(2,1)} %copy.118), calls=%async_computation.3 | async-start | bytes 65536 | tf_op jit(solution)/shard_map/all_to_all | solution.py:186
  381.6 7.4 %all-to-all-done.3 = bf16[8,16,96]{2,0,1:T(8,128)(2,1)} async-done(((bf16[8,16,96]{2,0,1:T(8,128)(2,1)}), bf16[8,16,96]{2,0,1:T(8,128)(2,1)}, u32[]{:S(2)}, u32[]{:S(2)}) %all-to-all-start.3) | async-done | bytes 24608 | tf_op jit(solution)/shard_map/all_to_all | solution.py:186
  389.1 3.9 all-to-all-start.4
  393.0 12.2 %all-to-all-done.4 = bf16[32,4,96]{2,1,0:T(4,128)(2,1)S(1)} async-done(((bf16[32,4,96]{2,1,0:T(4,128)(2,1)}), bf16[32,4,96]{2,1,0:T(4,128)(2,1)S(1)}, u32[]{:S(2)}, u32[]{:S(2)}) %all-to-all-start.4) | async-done | bytes 24608 | tf_op jit(solution)/shard_map/all_to_all | solution.py:189
  (111 shorter events, 25.3 us)
Async XLA Ops:
  7.2 367.8 %copy-start = (bf16[1,1536,1024]{2,1,0:T(8,128)(2,1)S(1)}, bf16[1,1536,1024]{2,1,0:T(8,128)(2,1)}, u32[]{:S(2)}) copy-start(bf16[1,1536,1024]{2,1,0:T(8,128)(2,1)} %param.24) | copy-start | bytes 9437188
  7.2 85.1 %all-gather.2.cloned.1.call-start = ((), (), s32[]{:S(2)}) async-start(), calls=%async_computation.5 | async-start | bytes 3342336 | tf_op jit(solution)/shard_map/all_gather | solution.py:34
  7.2 9.6 %collective-permute-start = (bf16[8,1536]{1,0:T(8,128)(2,1)}, bf16[8,1536]{1,0:T(8,128)(2,1)S(1)}, u32[]{:S(2)}, u32[]{:S(2)}) collective-permute-start(bf16[8,1536]{1,0:T(8,128)(2,1)} %param.16), channel_id=1, source_target_pairs={{0,16},{16,0},{32,48},{48,32},{64,80},{80,64},{96,112},{112,96},{1... | collective-permute-start | bytes 73736 | tf_op jit(solution)/shard_map/ppermute | solution.py:30
  31.3 95.7 %copy-start.5 = (bf16[8,2,512]{2,1,0:T(2,128)(2,1)S(1)}, bf16[8,2,512]{2,1,0:T(2,128)(2,1)}, u32[]{:S(2)}) copy-start(bf16[8,2,512]{2,1,0:T(2,128)(2,1)} %param.17) | copy-start | bytes 49156
  31.3 95.8 %copy-start.4 = (f32[8,8,3]{0,2,1:T(4,128)S(1)}, f32[8,8,3]{0,2,1:T(4,128)}, u32[]{:S(2)}) copy-start(f32[8,8,3]{0,2,1:T(4,128)} %bitcast_multiply_fusion.3) | copy-start | bytes 2308
  80.5 0.6 copy-start.2
  93.2 53.6 %copy-start.6 = (s32[8,8]{1,0:T(8,128)S(1)}, s32[8,8]{1,0:T(8,128)}, u32[]{:S(2)}) copy-start(s32[8,8]{1,0:T(8,128)} %param.26) | copy-start | bytes 772
  93.3 95.1 %copy-start.7 = (bf16[48,96]{1,0:T(8,128)(2,1)S(1)}, bf16[48,96]{1,0:T(8,128)(2,1)}, u32[]{:S(2)}) copy-start(bf16[48,96]{1,0:T(8,128)(2,1)} %param.22) | copy-start | bytes 27652
  93.3 187.3 %copy-start.8 = (bf16[8,96]{1,0:T(8,128)(2,1)S(1)}, bf16[8,96]{1,0:T(8,128)(2,1)}, u32[]{:S(2)}) copy-start(bf16[8,96]{1,0:T(8,128)(2,1)} %param.15) | copy-start | bytes 4612
  93.3 252.3 %copy-start.10 = (f32[96]{0:T(128)S(1)}, f32[96]{0:T(128)}, u32[]{:S(2)}) copy-start(f32[96]{0:T(128)} %param.23) | copy-start | bytes 1156
  121.6 7.9 %collective-permute-start.1 = (f32[8,24]{0,1:T(8,128)S(1)}, f32[8,24]{0,1:T(8,128)S(1)}, u32[]{:S(2)}, u32[]{:S(2)}) collective-permute-start(f32[8,24]{0,1:T(8,128)S(1)} %slice.47), channel_id=1, source_target_pairs={{0,16},{16,0},{32,48},{48,32},{64,80},{80,64},{96,112},{112,96},{1... | collective-permute-start | bytes 2312 | tf_op jit(solution)/shard_map/ppermute | solution.py:30
  123.9 5.5 %collective-permute-start.3 = (f32[8,24]{0,1:T(8,128)S(1)}, f32[8,24]{0,1:T(8,128)S(1)}, u32[]{:S(2)}, u32[]{:S(2)}) collective-permute-start(f32[8,24]{0,1:T(8,128)S(1)} %slice.50), channel_id=1, source_target_pairs={{0,16},{16,0},{32,48},{48,32},{64,80},{80,64},{96,112},{112,96},{1... | collective-permute-start | bytes 2312 | tf_op jit(solution)/shard_map/ppermute | solution.py:30
  127.3 5.4 %collective-permute-start.2 = (f32[8,24,64]{2,0,1:T(8,128)S(1)}, f32[8,24,64]{2,0,1:T(8,128)S(1)}, u32[]{:S(2)}, u32[]{:S(2)}) collective-permute-start(f32[8,24,64]{2,0,1:T(8,128)S(1)} %slice.48), channel_id=1, source_target_pairs={{0,16},{16,0},{32,48},{48,32},{64,80},{80,64},{96,112},{112,96},{1... | collective-permute-start | bytes 147464 | tf_op jit(solution)/shard_map/ppermute | solution.py:30
  132.9 242.5 %copy-start.3 = (bf16[8,1536]{1,0:T(8,128)(2,1)}, bf16[8,1536]{1,0:T(8,128)(2,1)S(1)}, u32[]{:S(2)}) copy-start(bf16[8,1536]{1,0:T(8,128)(2,1)S(1)} %convert_element_type.64) | copy-start | bytes 73732
  133.9 54.5 %all-to-all-start = ((bf16[32,8,1536]{2,1,0:T(8,128)(2,1)}), bf16[32,8,1536]{2,1,0:T(8,128)(2,1)}, u32[]{:S(2)}, u32[]{:S(2)}) async-start(bf16[32,8,1536]{2,1,0:T(8,128)(2,1)} %stack.2), calls=%async_computation | async-start | bytes 1572864 | tf_op jit(solution)/shard_map/all_to_all | solution.py:19
  146.8 234.9 %copy-start.9 = (bf16[8,8]{1,0:T(8,128)(2,1)S(1)}, bf16[8,8]{1,0:T(8,128)(2,1)}, u32[]{:S(2)}) copy-start(bf16[8,8]{1,0:T(8,128)(2,1)} %param.27) | copy-start | bytes 388
  362.1 12.7 %all-to-all-start.2 = ((bf16[16,8,96]{2,1,0:T(8,128)(2,1)}), bf16[16,8,96]{2,1,0:T(8,128)(2,1)S(1)}, u32[]{:S(2)}, u32[]{:S(2)}) async-start(bf16[16,8,96]{2,1,0:T(8,128)(2,1)} %bitcast.19), calls=%async_computation.2 | async-start | bytes 65536 | tf_op jit(solution)/shard_map/all_to_all | solution.py:176
  374.9 1.4 copy-start.1
  377.4 11.7 %all-to-all-start.3 = ((bf16[8,16,96]{2,0,1:T(8,128)(2,1)}), bf16[8,16,96]{2,0,1:T(8,128)(2,1)}, u32[]{:S(2)}, u32[]{:S(2)}) async-start(bf16[8,16,96]{2,0,1:T(8,128)(2,1)} %copy.118), calls=%async_computation.3 | async-start | bytes 65536 | tf_op jit(solution)/shard_map/all_to_all | solution.py:186
  389.1 16.1 %all-to-all-start.4 = ((bf16[32,4,96]{2,1,0:T(4,128)(2,1)}), bf16[32,4,96]{2,1,0:T(4,128)(2,1)S(1)}, u32[]{:S(2)}, u32[]{:S(2)}) async-start(bf16[32,4,96]{2,1,0:T(4,128)(2,1)} %bitcast.24), calls=%async_computation.4 | async-start | bytes 65536 | tf_op jit(solution)/shard_map/all_to_all | solution.py:189
Sparse Core Ops, SparseCore 0:
  21.2 71.0 all-gather.1
